TPU v7x, 32 devices: a whole 2x2x4 slice. The times are simulated.
32 devices in a mesh: lat: 16 (over z, x, core), lon: 2 (over y).
Axes of the slice: x: 2, y: 2, z: 4, core: 2. Of those that a mesh axis runs over, the one named last changes fastest.
Arguments:
- state: bfloat16 [2, 96, 128, 256], P(None, 'lat', 'lon'), may hold values from -6 to 6
- upstream: bfloat16 [2, 96, 128, 256], P(None, 'lat', 'lon'), may hold values from -6 to 6
- first_kernel: bfloat16 [9, 256, 256], replicated, may hold values from -0.125 to 0.125
- second_kernel: bfloat16 [9, 256, 256], replicated, may hold values from -0.125 to 0.125
Outputs:
- output_state: bfloat16 [2, 96, 128, 256], P(None, 'lat', 'lon')
- state_grad: bfloat16 [2, 96, 128, 256], P(None, 'lat', 'lon')
- first_grad: float32 [9, 256, 256], P(None, 'lat', 'lon')
- second_grad: float32 [9, 256, 256], P(None, 'lat', 'lon')
All inputs are finite; a program needn't handle non-finite values.
Results may differ from a plain program's by a relative error of at most 0.0033.
Values may be sent and summed in bfloat16 or wider, within the bound.
A program may use at most 64 MiB of HBM per device.

v0:
```python
import math
import jax
import jax.numpy as jnp
from jax import lax
from jax.sharding import PartitionSpec as P


def with_halo(array, sides, width, wrap):
    for axis, dim in sides:
        size, length = (lax.axis_size(axis), array.shape[dim])
        up = [(i, (i + 1) % size) for i in range(size if wrap else size - 1)]
        down = [(j, i) for i, j in up]
        last = lax.slice_in_dim(array, length - width, length, axis=dim)
        leading = lax.slice_in_dim(array, 0, width, axis=dim)
        before = lax.ppermute(last, axis, up)
        after = lax.ppermute(leading, axis, down)
        array = jnp.concatenate([before, array, after], axis=dim)
    return array


def pad_cycle(stacked):
    wide = with_halo(stacked, (("lon", 3),), 1, True)
    return with_halo(wide, (("lat", 2),), 1, False)


def conv_taps(padded, kernel, flipped):
    band_rows = padded.shape[1] - 2
    band_cols = padded.shape[2] - 2
    total = jnp.zeros((padded.shape[0], band_rows, band_cols, kernel.shape[2]), jnp.float32)
    for row_off in range(3):
        for col_off in range(3):
            window = padded[:, row_off : row_off + band_rows, col_off : col_off + band_cols, :]
            if flipped:
                total = total + jnp.einsum(
                    "bijd,cd->bijc",
                    window,
                    kernel[8 - 3 * row_off - col_off],
                    preferred_element_type=jnp.float32,
                )
            else:
                total = total + jnp.einsum(
                    "bijc,cd->bijd",
                    window,
                    kernel[3 * row_off + col_off],
                    preferred_element_type=jnp.float32,
                )
    return total


def kernel_terms(padded, grad_field):
    band_rows = grad_field.shape[1]
    band_cols = grad_field.shape[2]
    result = []
    for row_off in range(3):
        for col_off in range(3):
            window = padded[:, row_off : row_off + band_rows, col_off : col_off + band_cols, :]
            result.append(
                jnp.einsum("bijc,bijd->cd", window, grad_field, preferred_element_type=jnp.float32)
            )
    return jnp.stack(result)


def sum_lat(terms):
    moved = (
        lax.all_to_all(terms[0][None], "lat", split_axis=2, concat_axis=0, tiled=True),
        lax.all_to_all(terms[1][None], "lat", split_axis=2, concat_axis=0, tiled=True),
    )
    return (jnp.sum(moved[0], axis=0), jnp.sum(moved[1], axis=0))


def sum_lon(terms):
    moved = (
        lax.all_to_all(terms[0][None], "lon", split_axis=3, concat_axis=0, tiled=True),
        lax.all_to_all(terms[1][None], "lon", split_axis=3, concat_axis=0, tiled=True),
    )
    return (jnp.sum(moved[0], axis=0), jnp.sum(moved[1], axis=0))


def body(state, upstream, first_kernel, second_kernel):
    band_rows = state.shape[1]
    band_cols = state.shape[2]
    scale_factor = 1.0 / math.sqrt(
        band_rows * lax.axis_size("lat") * band_cols * lax.axis_size("lon")
    )
    both_pad = pad_cycle(jnp.stack([state, upstream]))
    state_pad = both_pad[0]
    upstream_pad = both_pad[1]
    pre = conv_taps(state_pad, first_kernel, False)
    active = jax.nn.silu(pre).astype(jnp.bfloat16)
    active_pad = pad_cycle(active[None])[0]
    second_out = conv_taps(active_pad, second_kernel, False)
    output_state = (state.astype(jnp.float32) + second_out).astype(jnp.bfloat16)
    back_act = conv_taps(upstream_pad, second_kernel, True)
    sigma = jax.nn.sigmoid(pre)
    back_pre = (back_act * sigma * (1.0 + pre * (1.0 - sigma))).astype(jnp.bfloat16)
    back_pad = pad_cycle(back_pre[None])[0]
    state_grad = (upstream.astype(jnp.float32) + conv_taps(back_pad, first_kernel, True)).astype(
        jnp.bfloat16
    )
    terms = (
        kernel_terms(state_pad, back_pre) * scale_factor,
        kernel_terms(active_pad, upstream) * scale_factor,
    )
    summed = sum_lon(sum_lat(terms))
    return (output_state, state_grad, summed[0], summed[1])


def solution(mesh):
    placed = (P(None, "lat", "lon", None), P(None, "lat", "lon", None), P(), P())
    return jax.shard_map(
        body,
        mesh=mesh,
        in_specs=placed,
        out_specs=(
            P(None, "lat", "lon", None),
            P(None, "lat", "lon", None),
            P(None, "lat", "lon"),
            P(None, "lat", "lon"),
        ),
        check_vma=False,
    )
```

profile of v0, /device:TPU:20, one launch (start us, length us, event | category | flops | bytes accessed | tf_op | source)
XLA Modules:
  0.0 192.8 jit_solution(8814331763132578597)
XLA Ops:
  2.2 1.5 collective-permute-start
  3.7 1.8 collective-permute-done.1
  7.1 1.9 collective-permute-start.3
  9.0 2.4 %collective-permute-start.2 = (bf16[2,2,1,66,256]{4,3,2,1,0:T(8,128)(2,1)S(1)}, bf16[2,2,1,66,256]{4,3,2,1,0:T(8,128)(2,1)S(1)}, u32[]{:S(2)}, u32[]{:S(2)}) collective-permute-start(bf16[2,2,1,66,256]{4,3,2,1,0:T(8,128)(2,1)S(1)} %get-tuple-element.14), channel_id=1, source_target_pairs={{0,2},{2,4},{4,6},{6,8},{8,10},{10,12},{12,14},{14,16},{16,18},{18... | collective-permute-start | bytes 405512 | tf_op jit(solution)/shard_map/ppermute | solution.py:15
  11.7 4.7 %collective-permute-done.2 = bf16[2,2,1,66,256]{4,3,2,1,0:T(8,128)(2,1)S(1)} collective-permute-done((bf16[2,2,1,66,256]{4,3,2,1,0:T(8,128)(2,1)S(1)}, bf16[2,2,1,66,256]{4,3,2,1,0:T(8,128)(2,1)S(1)}, u32[]{:S(2)}, u32[]{:S(2)}) %collective-permute-start.2) | collective-permute-done | bytes 135200 | tf_op jit(solution)/shard_map/ppermute | solution.py:15
  27.7 3.9 %copy.16 = f32[1,9,256,256]{3,0,1,2:T(1,128)} copy(f32[1,9,256,256]{3,2,1,0:T(8,128)S(1)} %broadcast_multiply_fusion.1) | data formatting | bytes 4718592 | tf_op jit(solution)/shard_map/mul | solution.py:101
  31.6 5.3 %all-to-all-start = ((f32[1,9,256,256]{3,0,1,2:T(1,128)}), f32[1,9,256,256]{3,0,1,2:T(1,128)S(1)}, u32[]{:S(2)}, u32[]{:S(2)}) async-start(f32[1,9,256,256]{3,0,1,2:T(1,128)} %copy.16), calls=%async_computation | async-start | bytes 4718592 | tf_op jit(solution)/shard_map/all_to_all | solution.py:65
  37.1 1.6 collective-permute-start.5
  39.2 1.6 collective-permute-start.9
  42.4 2.0 %collective-permute-start.7 = (bf16[1,2,1,66,256]{4,3,2,1,0:T(8,128)(2,1)S(1)}, bf16[1,2,1,66,256]{4,3,2,1,0:T(8,128)(2,1)S(1)}, u32[]{:S(2)}, u32[]{:S(2)}) collective-permute-start(bf16[1,2,1,66,256]{4,3,2,1,0:T(8,128)(2,1)S(1)} %get-tuple-element.21), channel_id=1, source_target_pairs={{2,0},{4,2},{6,4},{8,6},{10,8},{12,10},{14,12},{16,14},{18,16},{20... | collective-permute-start | bytes 202760 | tf_op jit(solution)/shard_map/ppermute | solution.py:16
  44.4 2.4 %collective-permute-start.6 = (bf16[1,2,1,66,256]{4,3,2,1,0:T(8,128)(2,1)S(1)}, bf16[1,2,1,66,256]{4,3,2,1,0:T(8,128)(2,1)S(1)}, u32[]{:S(2)}, u32[]{:S(2)}) collective-permute-start(bf16[1,2,1,66,256]{4,3,2,1,0:T(8,128)(2,1)S(1)} %get-tuple-element.20), channel_id=1, source_target_pairs={{0,2},{2,4},{4,6},{6,8},{8,10},{10,12},{12,14},{14,16},{16,18},{18... | collective-permute-start | bytes 202760 | tf_op jit(solution)/shard_map/ppermute | solution.py:15
  47.5 4.1 %collective-permute-start.11 = (bf16[1,2,1,66,256]{4,3,2,1,0:T(8,128)(2,1)}, bf16[1,2,1,66,256]{4,3,2,1,0:T(8,128)(2,1)S(1)}, u32[]{:S(2)}, u32[]{:S(2)}) collective-permute-start(bf16[1,2,1,66,256]{4,3,2,1,0:T(8,128)(2,1)} %get-tuple-element.19), channel_id=1, source_target_pairs={{2,0},{4,2},{6,4},{8,6},{10,8},{12,10},{14,12},{16,14},{18,16},{20... | collective-permute-start | bytes 202760 | tf_op jit(solution)/shard_map/ppermute | solution.py:16
  51.6 2.1 %collective-permute-start.10 = (bf16[1,2,1,66,256]{4,3,2,1,0:T(8,128)(2,1)S(1)}, bf16[1,2,1,66,256]{4,3,2,1,0:T(8,128)(2,1)}, u32[]{:S(2)}, u32[]{:S(2)}) collective-permute-start(bf16[1,2,1,66,256]{4,3,2,1,0:T(8,128)(2,1)S(1)} %get-tuple-element.18), channel_id=1, source_target_pairs={{0,2},{2,4},{4,6},{6,8},{8,10},{10,12},{12,14},{14,16},{16,18},{18... | collective-permute-start | bytes 202760 | tf_op jit(solution)/shard_map/ppermute | solution.py:15
  53.7 35.3 %collective-permute-done.7 = bf16[1,2,1,66,256]{4,3,2,1,0:T(8,128)(2,1)S(1)} collective-permute-done((bf16[1,2,1,66,256]{4,3,2,1,0:T(8,128)(2,1)S(1)}, bf16[1,2,1,66,256]{4,3,2,1,0:T(8,128)(2,1)S(1)}, u32[]{:S(2)}, u32[]{:S(2)}) %collective-permute-start.7) | collective-permute-done | bytes 67616 | tf_op jit(solution)/shard_map/ppermute | solution.py:16
  89.0 1.9 collective-permute-done.6
  94.2 3.9 %copy.22 = f32[1,9,256,256]{3,0,1,2:T(1,128)} copy(f32[1,9,256,256]{3,2,1,0:T(8,128)S(1)} %broadcast_multiply_fusion) | data formatting | bytes 4718592 | tf_op jit(solution)/shard_map/mul | solution.py:102
  98.1 4.3 %all-to-all-start.2 = ((f32[1,9,256,256]{3,0,1,2:T(1,128)}), f32[1,9,256,256]{3,0,1,2:T(1,128)}, u32[]{:S(2)}, u32[]{:S(2)}) async-start(f32[1,9,256,256]{3,0,1,2:T(1,128)} %copy.22), calls=%async_computation.2 | async-start | bytes 4718592 | tf_op jit(solution)/shard_map/all_to_all | solution.py:66
  112.3 2.5 %copy.66 = f32[1,9,256,256]{3,1,2,0:T(8,128)} copy(f32[1,9,256,256]{3,0,1,2:T(1,128)S(1)} %all-to-all-done) | data formatting | bytes 4718592 | tf_op jit(solution)/shard_map/all_to_all | solution.py:65
  114.8 2.7 %reduce_sum.36 = f32[9,16,256]{2,0,1:T(8,128)S(1)} reduce(f32[9,16,16,256]{3,0,2,1:T(8,128)} %bitcast.349, f32[]{:T(128)} %constant.2.clone.1), dimensions={1}, to_apply=%region_0.1 | reduce | flops 552960 | bytes 2506756 | tf_op jit(solution)/shard_map/reduce_sum | solution.py:68
  117.5 2.1 %copy.19 = f32[1,9,16,256]{2,0,1,3:T(1,128)} copy(f32[1,9,16,256]{3,1,2,0:T(8,128)S(1)} %bitcast.366) | data formatting | bytes 294912 | tf_op jit(solution)/shard_map/broadcast_in_dim | solution.py:73
  120.2 4.9 %reduce.12 = f32[256,9,16]{2,1,0:T(8,128)S(1)} reduce(f32[256,9,1,16]{3,2,1,0:T(1,128)} %bitcast.361, f32[]{:T(128)} %broadcast.23), dimensions={2}, to_apply=%bitcast.327.reduce_sub_computation | reduce | bytes 294916
  126.2 29.4 %all-to-all-done.2 = f32[1,9,256,256]{3,0,1,2:T(1,128)} async-done(((f32[1,9,256,256]{3,0,1,2:T(1,128)}), f32[1,9,256,256]{3,0,1,2:T(1,128)}, u32[]{:S(2)}, u32[]{:S(2)}) %all-to-all-start.2) | async-done | bytes 2359328 | tf_op jit(solution)/shard_map/all_to_all | solution.py:66
  155.7 4.9 %all-to-all-start.1 = ((f32[2,1,18432]{2,1,0:T(1,128)}), f32[2,1,18432]{2,1,0:T(1,128)S(1)}, u32[]{:S(2)}, u32[]{:S(2)}) async-start(f32[2,1,18432]{2,1,0:T(1,128)} %reshape.308), calls=%async_computation.1 | async-start | bytes 294912 | tf_op jit(solution)/shard_map/all_to_all | solution.py:73
  160.6 2.4 %convolution_add_fusion.1 = f32[2,6,64,256]{3,2,1,0:T(8,128)} fusion(f32[2,6,64,256]{3,2,1,0:T(8,128)} %convolution_add_fusion.2, bf16[2,8,66,256]{3,2,1,0:T(8,128)(2,1)S(1)} %maximum_bitcast_fusion.1, bf16[9,256,256]{2,1,0:T(8,128)(2,1)} %param.6), kind=kOutput, calls=%fused_computation.2 | convolution fusion | flops 100859904 | bytes 2097152 | tf_op jit(solution)/shard_map/bijd,cd->bijc/dot_general | solution.py:34
  163.0 4.2 %copy.67 = f32[1,9,256,256]{3,1,2,0:T(8,128)} copy(f32[1,9,256,256]{3,0,1,2:T(1,128)} %all-to-all-done.2) | data formatting | bytes 4718592 | tf_op jit(solution)/shard_map/all_to_all | solution.py:66
  167.2 2.7 %reduce_sum.38 = f32[9,16,256]{2,0,1:T(8,128)S(1)} reduce(f32[9,16,16,256]{3,0,2,1:T(8,128)} %bitcast.350, f32[]{:T(128)} %constant.2.clone.1), dimensions={1}, to_apply=%region_2.3 | reduce | flops 552960 | bytes 2506756 | tf_op jit(solution)/shard_map/reduce_sum | solution.py:68
  169.9 2.1 %copy.25 = f32[1,9,16,256]{2,0,1,3:T(1,128)} copy(f32[1,9,16,256]{3,1,2,0:T(8,128)S(1)} %bitcast.367) | data formatting | bytes 294912 | tf_op jit(solution)/shard_map/broadcast_in_dim | solution.py:74
  172.0 4.9 %reduce.14 = f32[256,9,16]{2,1,0:T(8,128)S(1)} reduce(f32[256,9,1,16]{3,2,1,0:T(1,128)} %bitcast.362, f32[]{:T(128)} %broadcast.23), dimensions={2}, to_apply=%bitcast.329.reduce_sub_computation | reduce | bytes 294916
  178.1 3.7 %all-to-all-start.3 = ((f32[2,1,18432]{2,1,0:T(1,128)}), f32[2,1,18432]{2,1,0:T(1,128)S(1)}, u32[]{:S(2)}, u32[]{:S(2)}) async-start(f32[2,1,18432]{2,1,0:T(1,128)} %reshape.310), calls=%async_computation.3 | async-start | bytes 294912 | tf_op jit(solution)/shard_map/all_to_all | solution.py:74
  181.8 2.3 %fusion.6 = bf16[2,6,64,256]{3,2,1,0:T(8,128)(2,1)} fusion(f32[2,6,64,256]{3,2,1,0:T(8,128)} %convolution_add_fusion.1, bf16[2,6,64,256]{3,2,1,0:T(8,128)(2,1)S(1)} %copy-done.3, bf16[2,8,66,256]{3,2,1,0:T(8,128)(2,1)S(1)} %maximum_bitcast_fusion.1, bf16[9,256,256]{2,1,0:T(8,128)(2,1)} %param.6), kind=kOutput, calls=%fused_computation.38 | convolution fusion | flops 101449728 | bytes 2097152 | tf_op jit(solution)/shard_map/bijd,cd->bijc/dot_general | solution.py:34
  185.1 1.9 reshape.309
  189.5 1.9 reshape.311
  (114 shorter events, 38.1 us)
Async XLA Ops:
  0.6 15.7 %copy-start.2 = (bf16[2,6,64,256]{3,2,1,0:T(8,128)(2,1)S(1)}, bf16[2,6,64,256]{3,2,1,0:T(8,128)(2,1)}, u32[]{:S(2)}) copy-start(bf16[2,6,64,256]{3,2,1,0:T(8,128)(2,1)} %param.5) | copy-start | bytes 1179652
  0.6 15.7 %copy-start = (bf16[2,6,64,256]{3,2,1,0:T(8,128)(2,1)S(1)}, bf16[2,6,64,256]{3,2,1,0:T(8,128)(2,1)}, u32[]{:S(2)}) copy-start(bf16[2,6,64,256]{3,2,1,0:T(8,128)(2,1)} %param.4) | copy-start | bytes 1179652
  1.6 3.9 %collective-permute-start.1 = (bf16[2,2,6,1,256]{4,3,2,1,0:T(2,128)(2,1)S(1)}, bf16[2,2,6,1,256]{4,3,2,1,0:T(2,128)(2,1)S(1)}, u32[]{:S(2)}, u32[]{:S(2)}) collective-permute-start(bf16[2,2,6,1,256]{4,3,2,1,0:T(2,128)(2,1)S(1)} %get-tuple-element.17), channel_id=1, source_target_pairs={{1,0},{0,1},{3,2},{2,3},{5,4},{4,5},{7,6},{6,7},{9,8},{8,9},{11,10... | collective-permute-start | bytes 36872 | tf_op jit(solution)/shard_map/ppermute | solution.py:16
  2.2 3.8 %collective-permute-start = (bf16[2,2,6,1,256]{4,3,2,1,0:T(2,128)(2,1)S(1)}, bf16[2,2,6,1,256]{4,3,2,1,0:T(2,128)(2,1)S(1)}, u32[]{:S(2)}, u32[]{:S(2)}) collective-permute-start(bf16[2,2,6,1,256]{4,3,2,1,0:T(2,128)(2,1)S(1)} %get-tuple-element.16), channel_id=1, source_target_pairs={{0,1},{1,0},{2,3},{3,2},{4,5},{5,4},{6,7},{7,6},{8,9},{9,8},{10,11... | collective-permute-start | bytes 36872 | tf_op jit(solution)/shard_map/ppermute | solution.py:15
  7.1 4.6 %collective-permute-start.3 = (bf16[2,2,1,66,256]{4,3,2,1,0:T(8,128)(2,1)S(1)}, bf16[2,2,1,66,256]{4,3,2,1,0:T(8,128)(2,1)S(1)}, u32[]{:S(2)}, u32[]{:S(2)}) collective-permute-start(bf16[2,2,1,66,256]{4,3,2,1,0:T(8,128)(2,1)S(1)} %get-tuple-element.15), channel_id=1, source_target_pairs={{2,0},{4,2},{6,4},{8,6},{10,8},{12,10},{14,12},{16,14},{18,16},{20... | collective-permute-start | bytes 405512 | tf_op jit(solution)/shard_map/ppermute | solution.py:16
  9.0 7.4 %collective-permute-start.2 = (bf16[2,2,1,66,256]{4,3,2,1,0:T(8,128)(2,1)S(1)}, bf16[2,2,1,66,256]{4,3,2,1,0:T(8,128)(2,1)S(1)}, u32[]{:S(2)}, u32[]{:S(2)}) collective-permute-start(bf16[2,2,1,66,256]{4,3,2,1,0:T(8,128)(2,1)S(1)} %get-tuple-element.14), channel_id=1, source_target_pairs={{0,2},{2,4},{4,6},{6,8},{8,10},{10,12},{12,14},{14,16},{16,18},{18... | collective-permute-start | bytes 405512 | tf_op jit(solution)/shard_map/ppermute | solution.py:15
  16.9 1.3 copy-start.4
  20.4 1.3 copy-start.6
  24.6 2.6 %copy-start.8 = (bf16[2,6,64,256]{3,2,1,0:T(8,128)(2,1)}, bf16[2,6,64,256]{3,2,1,0:T(8,128)(2,1)S(1)}, u32[]{:S(2)}) copy-start(bf16[2,6,64,256]{3,2,1,0:T(8,128)(2,1)S(1)} %fusion.5) | copy-start | bytes 1179652
  31.6 66.5 %all-to-all-start = ((f32[1,9,256,256]{3,0,1,2:T(1,128)}), f32[1,9,256,256]{3,0,1,2:T(1,128)S(1)}, u32[]{:S(2)}, u32[]{:S(2)}) async-start(f32[1,9,256,256]{3,0,1,2:T(1,128)} %copy.16), calls=%async_computation | async-start | bytes 4718592 | tf_op jit(solution)/shard_map/all_to_all | solution.py:65
  36.8 2.4 %copy-start.9 = (bf16[2,6,64,256]{3,2,1,0:T(8,128)(2,1)S(1)}, bf16[2,6,64,256]{3,2,1,0:T(8,128)(2,1)}, u32[]{:S(2)}) copy-start(bf16[2,6,64,256]{3,2,1,0:T(8,128)(2,1)} %copy-done.8) | copy-start | bytes 1179652
  37.1 4.2 %collective-permute-start.5 = (bf16[1,2,6,1,256]{4,3,2,1,0:T(2,128)(2,1)S(1)}, bf16[1,2,6,1,256]{4,3,2,1,0:T(2,128)(2,1)S(1)}, u32[]{:S(2)}, u32[]{:S(2)}) collective-permute-start(bf16[1,2,6,1,256]{4,3,2,1,0:T(2,128)(2,1)S(1)} %get-tuple-element.25), channel_id=1, source_target_pairs={{1,0},{0,1},{3,2},{2,3},{5,4},{4,5},{7,6},{6,7},{9,8},{8,9},{11,10... | collective-permute-start | bytes 18440 | tf_op jit(solution)/shard_map/ppermute | solution.py:16
  38.7 3.7 %collective-permute-start.4 = (bf16[1,2,6,1,256]{4,3,2,1,0:T(2,128)(2,1)S(1)}, bf16[1,2,6,1,256]{4,3,2,1,0:T(2,128)(2,1)S(1)}, u32[]{:S(2)}, u32[]{:S(2)}) collective-permute-start(bf16[1,2,6,1,256]{4,3,2,1,0:T(2,128)(2,1)S(1)} %get-tuple-element.24), channel_id=1, source_target_pairs={{0,1},{1,0},{2,3},{3,2},{4,5},{5,4},{6,7},{7,6},{8,9},{9,8},{10,11... | collective-permute-start | bytes 18440 | tf_op jit(solution)/shard_map/ppermute | solution.py:15
  39.2 7.6 %collective-permute-start.9 = (bf16[1,2,6,1,256]{4,3,2,1,0:T(2,128)(2,1)S(1)}, bf16[1,2,6,1,256]{4,3,2,1,0:T(2,128)(2,1)S(1)}, u32[]{:S(2)}, u32[]{:S(2)}) collective-permute-start(bf16[1,2,6,1,256]{4,3,2,1,0:T(2,128)(2,1)S(1)} %get-tuple-element.23), channel_id=1, source_target_pairs={{1,0},{0,1},{3,2},{2,3},{5,4},{4,5},{7,6},{6,7},{9,8},{8,9},{11,10... | collective-permute-start | bytes 18440 | tf_op jit(solution)/shard_map/ppermute | solution.py:16
  40.8 6.0 %collective-permute-start.8 = (bf16[1,2,6,1,256]{4,3,2,1,0:T(2,128)(2,1)S(1)}, bf16[1,2,6,1,256]{4,3,2,1,0:T(2,128)(2,1)S(1)}, u32[]{:S(2)}, u32[]{:S(2)}) collective-permute-start(bf16[1,2,6,1,256]{4,3,2,1,0:T(2,128)(2,1)S(1)} %get-tuple-element.22), channel_id=1, source_target_pairs={{0,1},{1,0},{2,3},{3,2},{4,5},{5,4},{6,7},{7,6},{8,9},{9,8},{10,11... | collective-permute-start | bytes 18440 | tf_op jit(solution)/shard_map/ppermute | solution.py:15
  42.4 46.6 %collective-permute-start.7 = (bf16[1,2,1,66,256]{4,3,2,1,0:T(8,128)(2,1)S(1)}, bf16[1,2,1,66,256]{4,3,2,1,0:T(8,128)(2,1)S(1)}, u32[]{:S(2)}, u32[]{:S(2)}) collective-permute-start(bf16[1,2,1,66,256]{4,3,2,1,0:T(8,128)(2,1)S(1)} %get-tuple-element.21), channel_id=1, source_target_pairs={{2,0},{4,2},{6,4},{8,6},{10,8},{12,10},{14,12},{16,14},{18,16},{20... | collective-permute-start | bytes 202760 | tf_op jit(solution)/shard_map/ppermute | solution.py:16
  44.4 46.5 %collective-permute-start.6 = (bf16[1,2,1,66,256]{4,3,2,1,0:T(8,128)(2,1)S(1)}, bf16[1,2,1,66,256]{4,3,2,1,0:T(8,128)(2,1)S(1)}, u32[]{:S(2)}, u32[]{:S(2)}) collective-permute-start(bf16[1,2,1,66,256]{4,3,2,1,0:T(8,128)(2,1)S(1)} %get-tuple-element.20), channel_id=1, source_target_pairs={{0,2},{2,4},{4,6},{6,8},{8,10},{10,12},{12,14},{14,16},{16,18},{18... | collective-permute-start | bytes 202760 | tf_op jit(solution)/shard_map/ppermute | solution.py:15
  46.8 0.7 copy-start.11
  47.5 55.0 %collective-permute-start.11 = (bf16[1,2,1,66,256]{4,3,2,1,0:T(8,128)(2,1)}, bf16[1,2,1,66,256]{4,3,2,1,0:T(8,128)(2,1)S(1)}, u32[]{:S(2)}, u32[]{:S(2)}) collective-permute-start(bf16[1,2,1,66,256]{4,3,2,1,0:T(8,128)(2,1)} %get-tuple-element.19), channel_id=1, source_target_pairs={{2,0},{4,2},{6,4},{8,6},{10,8},{12,10},{14,12},{16,14},{18,16},{20... | collective-permute-start | bytes 202760 | tf_op jit(solution)/shard_map/ppermute | solution.py:16
  51.6 51.5 %collective-permute-start.10 = (bf16[1,2,1,66,256]{4,3,2,1,0:T(8,128)(2,1)S(1)}, bf16[1,2,1,66,256]{4,3,2,1,0:T(8,128)(2,1)}, u32[]{:S(2)}, u32[]{:S(2)}) collective-permute-start(bf16[1,2,1,66,256]{4,3,2,1,0:T(8,128)(2,1)S(1)} %get-tuple-element.18), channel_id=1, source_target_pairs={{0,2},{2,4},{4,6},{6,8},{8,10},{10,12},{12,14},{14,16},{16,18},{18... | collective-permute-start | bytes 202760 | tf_op jit(solution)/shard_map/ppermute | solution.py:15
  98.1 57.6 %all-to-all-start.2 = ((f32[1,9,256,256]{3,0,1,2:T(1,128)}), f32[1,9,256,256]{3,0,1,2:T(1,128)}, u32[]{:S(2)}, u32[]{:S(2)}) async-start(f32[1,9,256,256]{3,0,1,2:T(1,128)} %copy.22), calls=%async_computation.2 | async-start | bytes 4718592 | tf_op jit(solution)/shard_map/all_to_all | solution.py:66
  102.4 3.2 %copy-start.5 = (bf16[9,256,256]{2,1,0:T(8,128)(2,1)S(1)}, bf16[9,256,256]{2,1,0:T(8,128)(2,1)}, u32[]{:S(2)}) copy-start(bf16[9,256,256]{2,1,0:T(8,128)(2,1)} %param.6) | copy-start | bytes 3538948
  102.4 0.6 copy-start.10
  104.3 1.6 copy-start.7
  107.6 1.0 copy-start.1
  155.7 22.4 %all-to-all-start.1 = ((f32[2,1,18432]{2,1,0:T(1,128)}), f32[2,1,18432]{2,1,0:T(1,128)S(1)}, u32[]{:S(2)}, u32[]{:S(2)}) async-start(f32[2,1,18432]{2,1,0:T(1,128)} %reshape.308), calls=%async_computation.1 | async-start | bytes 294912 | tf_op jit(solution)/shard_map/all_to_all | solution.py:73
  177.0 4.8 %copy-start.3 = (bf16[2,6,64,256]{3,2,1,0:T(8,128)(2,1)S(1)}, bf16[2,6,64,256]{3,2,1,0:T(8,128)(2,1)}, u32[]{:S(2)}) copy-start(bf16[2,6,64,256]{3,2,1,0:T(8,128)(2,1)} %param.5) | copy-start | bytes 1179652
  178.1 10.3 %all-to-all-start.3 = ((f32[2,1,18432]{2,1,0:T(1,128)}), f32[2,1,18432]{2,1,0:T(1,128)S(1)}, u32[]{:S(2)}, u32[]{:S(2)}) async-start(f32[2,1,18432]{2,1,0:T(1,128)} %reshape.310), calls=%async_computation.3 | async-start | bytes 294912 | tf_op jit(solution)/shard_map/all_to_all | solution.py:74
where the time goes:
time: 194 us; the launch traced here: 193 us
  waiting for transfers between devices  74.9 us (39%)
  starting transfers between devices  39.3 us (20%)
  local copies, waits for them, and re-layouts  31.2 us (16%)
  other arithmetic  23.3 us (12%)
  matrix products  22.7 us (12%)
    ppermute x6, waiting for transfers between devices, with_halo(): after = lax.ppermute(leading, axis, down)  37.4 us
    all_to_all x1, waiting for transfers between devices, sum_lat(): lax.all_to_all(terms[1][None], 'lat', split_axis=2, concat_axis=0, tiled=...  29.4 us
    unnamed x33, local copies, waits for them, and re-layouts  12.3 us
    ppermute x6, starting transfers between devices, with_halo(): after = lax.ppermute(leading, axis, down)  11.8 us
    dot_general x18, matrix products, conv_taps(): jnp.einsum('bijd,cd->bijc', window, kernel[8 - 3 * row_off - col_off], pr...  10.5 us
    unnamed x2, other arithmetic  9.8 us
    ppermute x6, starting transfers between devices, with_halo(): before = lax.ppermute(last, axis, up)  9.37 us
    ppermute x6, waiting for transfers between devices, with_halo(): before = lax.ppermute(last, axis, up)  8.16 us
  transfers between devices with their start and end apart: 16, of which 8 were waited for; matrix products, arithmetic and copies ran while one was open for 28% of the time, Pallas kernels for 0%

commit v1 on v0

--- a/solution.py
+++ b/solution.py
@@ -1,8 +1,19 @@
+import functools
 import math
 import jax
 import jax.numpy as jnp
 from jax import lax
 from jax.sharding import PartitionSpec as P
+
+
+def bind_paths(arr_in, dev_axis):
+    local_now = lax.axis_size(dev_axis)
+    field_out = jnp.split(arr_in, local_now, 2)
+    high = lax.all_to_all(jnp.stack(field_out, axis=0), dev_axis, 0, 0)
+    return jnp.concatenate(high, axis=0)
+
+
+obtain_local_data = functools.partial(bind_paths, dev_axis="lat")
 
 
 def with_halo(array, sides, width, wrap):
@@ -63,7 +74,7 @@
 def sum_lat(terms):
     moved = (
         lax.all_to_all(terms[0][None], "lat", split_axis=2, concat_axis=0, tiled=True),
-        lax.all_to_all(terms[1][None], "lat", split_axis=2, concat_axis=0, tiled=True),
+        obtain_local_data(terms[1][None]),
     )
     return (jnp.sum(moved[0], axis=0), jnp.sum(moved[1], axis=0))
 

time: 194 us -> 203 us (1.046)
  other arithmetic: 23.3 us -> 27.4 us
  starting transfers between devices: 39.3 us -> 42 us
  waiting for transfers between devices: 74.9 us -> 77.6 us
    unnamed x33 -> x48, local copies, waits for them, and re-layouts: 12.3 us -> 19.9 us
    all_to_all x1 -> x0, local copies, waits for them, and re-layouts: 4.2 us -> none  [sum_lat(): lax.all_to_all(terms[1][None], 'lat', split_axis=2, concat_axis=0, tiled=...]
    mul x1 -> x0, local copies, waits for them, and re-layouts: 3.91 us -> none  [body(): kernel_terms(active_pad, upstream) * scale_factor]
    ppermute x6, waiting for transfers between devices: 37.4 us -> 40.9 us  [with_halo(): after = lax.ppermute(leading, axis, down)]
  transfers between devices with their start and end apart: 16 -> 16, of which waited for: 8 -> 7; matrix products, arithmetic and copies ran while one was open for 28% -> 34% of each run, Pallas kernels for 0% -> 0%
where the time goes in v1:
time: 203 us; the launch traced here: 202 us
  waiting for transfers between devices  77.6 us (38%)
  starting transfers between devices  42 us (21%)
  local copies, waits for them, and re-layouts  31.3 us (15%)
  other arithmetic  27.4 us (13%)
  matrix products  22.4 us (11%)
    ppermute x6, waiting for transfers between devices, with_halo(): after = lax.ppermute(leading, axis, down)  40.9 us
    all_to_all x1, waiting for transfers between devices, bind_paths(): high = lax.all_to_all(jnp.stack(field_out, axis=0), dev_axis, 0, 0)  29.6 us
    unnamed x48, local copies, waits for them, and re-layouts  19.9 us
    ppermute x6, starting transfers between devices, with_halo(): after = lax.ppermute(leading, axis, down)  13.4 us
    dot_general x18, matrix products, conv_taps(): jnp.einsum('bijd,cd->bijc', window, kernel[8 - 3 * row_off - col_off], pr...  10.3 us
    unnamed x2, other arithmetic  9.93 us
    ppermute x6, starting transfers between devices, with_halo(): before = lax.ppermute(last, axis, up)  8.98 us
    ppermute x6, waiting for transfers between devices, with_halo(): before = lax.ppermute(last, axis, up)  7.04 us
  transfers between devices with their start and end apart: 16, of which 7 were waited for; matrix products, arithmetic and copies ran while one was open for 34% of the time, Pallas kernels for 0%

profile of v1, /device:TPU:20, one launch (start us, length us, event | category | flops | bytes accessed | tf_op | source)
XLA Modules:
  0.0 201.9 jit_solution(8849661104267004494)
XLA Ops:
  3.6 1.8 collective-permute-done.1
  7.0 2.1 %collective-permute-start.3 = (bf16[2,2,1,66,256]{4,3,2,1,0:T(8,128)(2,1)S(1)}, bf16[2,2,1,66,256]{4,3,2,1,0:T(8,128)(2,1)S(1)}, u32[]{:S(2)}, u32[]{:S(2)}) collective-permute-start(bf16[2,2,1,66,256]{4,3,2,1,0:T(8,128)(2,1)S(1)} %get-tuple-element.15), channel_id=1, source_target_pairs={{2,0},{4,2},{6,4},{8,6},{10,8},{12,10},{14,12},{16,14},{18,16},{20... | collective-permute-start | bytes 405512 | tf_op jit(solution)/shard_map/ppermute | solution.py:27
  9.1 2.4 %collective-permute-start.2 = (bf16[2,2,1,66,256]{4,3,2,1,0:T(8,128)(2,1)S(1)}, bf16[2,2,1,66,256]{4,3,2,1,0:T(8,128)(2,1)S(1)}, u32[]{:S(2)}, u32[]{:S(2)}) collective-permute-start(bf16[2,2,1,66,256]{4,3,2,1,0:T(8,128)(2,1)S(1)} %get-tuple-element.14), channel_id=1, source_target_pairs={{0,2},{2,4},{4,6},{6,8},{8,10},{10,12},{12,14},{14,16},{16,18},{18... | collective-permute-start | bytes 405512 | tf_op jit(solution)/shard_map/ppermute | solution.py:26
  11.7 4.7 %collective-permute-done.2 = bf16[2,2,1,66,256]{4,3,2,1,0:T(8,128)(2,1)S(1)} collective-permute-done((bf16[2,2,1,66,256]{4,3,2,1,0:T(8,128)(2,1)S(1)}, bf16[2,2,1,66,256]{4,3,2,1,0:T(8,128)(2,1)S(1)}, u32[]{:S(2)}, u32[]{:S(2)}) %collective-permute-start.2) | collective-permute-done | bytes 135200 | tf_op jit(solution)/shard_map/ppermute | solution.py:26
  16.4 1.7 pad_maximum_fusion
  21.0 1.6 collective-permute-start.5
  26.4 1.6 collective-permute-start.9
  31.3 3.9 %copy.14 = f32[1,9,256,256]{3,0,1,2:T(1,128)} copy(f32[1,9,256,256]{3,2,1,0:T(8,128)S(1)} %broadcast_multiply_fusion.1) | data formatting | bytes 4718592 | tf_op jit(solution)/shard_map/mul | solution.py:112
  35.2 5.4 %all-to-all-start = ((f32[1,9,256,256]{3,0,1,2:T(1,128)}), f32[1,9,256,256]{3,0,1,2:T(1,128)S(1)}, u32[]{:S(2)}, u32[]{:S(2)}) async-start(f32[1,9,256,256]{3,0,1,2:T(1,128)} %copy.14), calls=%async_computation | async-start | bytes 4718592 | tf_op jit(solution)/shard_map/all_to_all | solution.py:76
  40.6 3.1 %collective-permute-start.7 = (bf16[1,2,1,66,256]{4,3,2,1,0:T(8,128)(2,1)S(1)}, bf16[1,2,1,66,256]{4,3,2,1,0:T(8,128)(2,1)S(1)}, u32[]{:S(2)}, u32[]{:S(2)}) collective-permute-start(bf16[1,2,1,66,256]{4,3,2,1,0:T(8,128)(2,1)S(1)} %get-tuple-element.21), channel_id=1, source_target_pairs={{2,0},{4,2},{6,4},{8,6},{10,8},{12,10},{14,12},{16,14},{18,16},{20... | collective-permute-start | bytes 202760 | tf_op jit(solution)/shard_map/ppermute | solution.py:27
  43.7 1.9 collective-permute-start.6
  47.3 4.5 %collective-permute-start.11 = (bf16[1,2,1,66,256]{4,3,2,1,0:T(8,128)(2,1)}, bf16[1,2,1,66,256]{4,3,2,1,0:T(8,128)(2,1)S(1)}, u32[]{:S(2)}, u32[]{:S(2)}) collective-permute-start(bf16[1,2,1,66,256]{4,3,2,1,0:T(8,128)(2,1)} %get-tuple-element.19), channel_id=1, source_target_pairs={{2,0},{4,2},{6,4},{8,6},{10,8},{12,10},{14,12},{16,14},{18,16},{20... | collective-permute-start | bytes 202760 | tf_op jit(solution)/shard_map/ppermute | solution.py:27
  51.8 2.1 %collective-permute-start.10 = (bf16[1,2,1,66,256]{4,3,2,1,0:T(8,128)(2,1)S(1)}, bf16[1,2,1,66,256]{4,3,2,1,0:T(8,128)(2,1)}, u32[]{:S(2)}, u32[]{:S(2)}) collective-permute-start(bf16[1,2,1,66,256]{4,3,2,1,0:T(8,128)(2,1)S(1)} %get-tuple-element.18), channel_id=1, source_target_pairs={{0,2},{2,4},{4,6},{6,8},{8,10},{10,12},{12,14},{14,16},{16,18},{18... | collective-permute-start | bytes 202760 | tf_op jit(solution)/shard_map/ppermute | solution.py:26
  53.9 38.9 %collective-permute-done.7 = bf16[1,2,1,66,256]{4,3,2,1,0:T(8,128)(2,1)S(1)} collective-permute-done((bf16[1,2,1,66,256]{4,3,2,1,0:T(8,128)(2,1)S(1)}, bf16[1,2,1,66,256]{4,3,2,1,0:T(8,128)(2,1)S(1)}, u32[]{:S(2)}, u32[]{:S(2)}) %collective-permute-start.7) | collective-permute-done | bytes 67616 | tf_op jit(solution)/shard_map/ppermute | solution.py:27
  92.8 1.8 collective-permute-done.6
  109.5 4.3 %all-to-all-start.2 = ((f32[16,1,9,16,256]{4,3,2,1,0:T(8,128)}), f32[16,1,9,16,256]{4,3,2,1,0:T(8,128)}, u32[]{:S(2)}, u32[]{:S(2)}) async-start(f32[16,1,9,16,256]{4,3,2,1,0:T(8,128)} %fusion.84), calls=%async_computation.2 | async-start | bytes 4718592 | tf_op jit(solution)/shard_map/all_to_all | solution.py:12
  123.5 2.5 %copy.61 = f32[1,9,256,256]{3,1,2,0:T(8,128)} copy(f32[1,9,256,256]{3,0,1,2:T(1,128)S(1)} %all-to-all-done) | data formatting | bytes 4718592 | tf_op jit(solution)/shard_map/all_to_all | solution.py:76
  126.0 2.7 %reduce_sum.36 = f32[9,16,256]{2,0,1:T(8,128)S(1)} reduce(f32[9,16,16,256]{3,0,2,1:T(8,128)} %bitcast.411, f32[]{:T(128)} %constant.2.clone.1), dimensions={1}, to_apply=%region_0.1 | reduce | flops 552960 | bytes 2506756 | tf_op jit(solution)/shard_map/reduce_sum | solution.py:79
  128.7 2.1 %copy.17 = f32[1,9,16,256]{2,0,1,3:T(1,128)} copy(f32[1,9,16,256]{3,1,2,0:T(8,128)S(1)} %bitcast.427) | data formatting | bytes 294912 | tf_op jit(solution)/shard_map/broadcast_in_dim | solution.py:84
  131.4 5.0 %reduce.10 = f32[256,9,16]{2,1,0:T(8,128)S(1)} reduce(f32[256,9,1,16]{3,2,1,0:T(1,128)} %bitcast.422, f32[]{:T(128)} %broadcast.23), dimensions={2}, to_apply=%bitcast.389.reduce_sub_computation | reduce | bytes 294916
  137.5 29.6 %all-to-all-done.2 = f32[16,1,9,16,256]{4,3,2,1,0:T(8,128)} async-done(((f32[16,1,9,16,256]{4,3,2,1,0:T(8,128)}), f32[16,1,9,16,256]{4,3,2,1,0:T(8,128)}, u32[]{:S(2)}, u32[]{:S(2)}) %all-to-all-start.2) | async-done | bytes 2359328 | tf_op jit(solution)/shard_map/all_to_all | solution.py:12
  167.1 5.6 %all-to-all-start.1 = ((f32[2,1,18432]{2,1,0:T(1,128)}), f32[2,1,18432]{2,1,0:T(1,128)}, u32[]{:S(2)}, u32[]{:S(2)}) async-start(f32[2,1,18432]{2,1,0:T(1,128)} %reshape.308), calls=%async_computation.1 | async-start | bytes 294912 | tf_op jit(solution)/shard_map/all_to_all | solution.py:84
  172.7 2.1 %convolution_add_fusion.1 = f32[2,6,64,256]{3,2,1,0:T(8,128)} fusion(f32[2,6,64,256]{3,2,1,0:T(8,128)S(1)} %copy-done.8, bf16[2,8,66,256]{3,2,1,0:T(8,128)(2,1)S(1)} %maximum_bitcast_fusion.1, bf16[9,256,256]{2,1,0:T(8,128)(2,1)} %param.6), kind=kOutput, calls=%fused_computation.2 | convolution fusion | flops 100859904 | bytes 2097152 | tf_op jit(solution)/shard_map/bijd,cd->bijc/dot_general | solution.py:45
  174.8 1.9 reduce_sum.38
  176.7 2.1 %copy.20 = f32[1,9,16,256]{2,0,1,3:T(1,128)} copy(f32[1,9,16,256]{3,2,1,0:T(8,128)S(1)} %bitcast.428) | data formatting | bytes 294912 | tf_op jit(solution)/shard_map/broadcast_in_dim | solution.py:85
  178.8 5.0 %reduce.12 = f32[256,9,16]{2,1,0:T(8,128)S(1)} reduce(f32[256,9,1,16]{3,2,1,0:T(1,128)} %bitcast.423, f32[]{:T(128)} %broadcast.23), dimensions={2}, to_apply=%bitcast.391.reduce_sub_computation | reduce | bytes 294916
  184.9 4.3 %all-to-all-start.3 = ((f32[2,1,18432]{2,1,0:T(1,128)}), f32[2,1,18432]{2,1,0:T(1,128)}, u32[]{:S(2)}, u32[]{:S(2)}) async-start(f32[2,1,18432]{2,1,0:T(1,128)} %reshape.310), calls=%async_computation.3 | async-start | bytes 294912 | tf_op jit(solution)/shard_map/all_to_all | solution.py:85
  189.1 2.3 %fusion.6 = bf16[2,6,64,256]{3,2,1,0:T(8,128)(2,1)} fusion(f32[2,6,64,256]{3,2,1,0:T(8,128)} %convolution_add_fusion.1, bf16[2,6,64,256]{3,2,1,0:T(8,128)(2,1)S(1)} %copy-done.2, bf16[2,8,66,256]{3,2,1,0:T(8,128)(2,1)S(1)} %maximum_bitcast_fusion.1, bf16[9,256,256]{2,1,0:T(8,128)(2,1)} %param.6), kind=kOutput, calls=%fused_computation.38 | convolution fusion | flops 101449728 | bytes 2097152 | tf_op jit(solution)/shard_map/bijd,cd->bijc/dot_general | solution.py:45
  191.4 2.0 reduce.11
  193.4 1.9 reshape.309
  196.7 2.0 reduce.13
  198.7 1.9 reshape.311
  (128 shorter events, 46.0 us)
Async XLA Ops:
  1.6 3.9 %collective-permute-start.1 = (bf16[2,2,6,1,256]{4,3,2,1,0:T(2,128)(2,1)S(1)}, bf16[2,2,6,1,256]{4,3,2,1,0:T(2,128)(2,1)S(1)}, u32[]{:S(2)}, u32[]{:S(2)}) collective-permute-start(bf16[2,2,6,1,256]{4,3,2,1,0:T(2,128)(2,1)S(1)} %get-tuple-element.17), channel_id=1, source_target_pairs={{1,0},{0,1},{3,2},{2,3},{5,4},{4,5},{7,6},{6,7},{9,8},{8,9},{11,10... | collective-permute-start | bytes 36872 | tf_op jit(solution)/shard_map/ppermute | solution.py:27
  2.1 3.8 %collective-permute-start = (bf16[2,2,6,1,256]{4,3,2,1,0:T(2,128)(2,1)S(1)}, bf16[2,2,6,1,256]{4,3,2,1,0:T(2,128)(2,1)S(1)}, u32[]{:S(2)}, u32[]{:S(2)}) collective-permute-start(bf16[2,2,6,1,256]{4,3,2,1,0:T(2,128)(2,1)S(1)} %get-tuple-element.16), channel_id=1, source_target_pairs={{0,1},{1,0},{2,3},{3,2},{4,5},{5,4},{6,7},{7,6},{8,9},{9,8},{10,11... | collective-permute-start | bytes 36872 | tf_op jit(solution)/shard_map/ppermute | solution.py:26
  7.0 11.2 %copy-start.3 = (bf16[9,256,256]{2,1,0:T(8,128)(2,1)S(1)}, bf16[9,256,256]{2,1,0:T(8,128)(2,1)}, u32[]{:S(2)}) copy-start(bf16[9,256,256]{2,1,0:T(8,128)(2,1)} %param.6) | copy-start | bytes 3538948
  7.0 4.7 %collective-permute-start.3 = (bf16[2,2,1,66,256]{4,3,2,1,0:T(8,128)(2,1)S(1)}, bf16[2,2,1,66,256]{4,3,2,1,0:T(8,128)(2,1)S(1)}, u32[]{:S(2)}, u32[]{:S(2)}) collective-permute-start(bf16[2,2,1,66,256]{4,3,2,1,0:T(8,128)(2,1)S(1)} %get-tuple-element.15), channel_id=1, source_target_pairs={{2,0},{4,2},{6,4},{8,6},{10,8},{12,10},{14,12},{16,14},{18,16},{20... | collective-permute-start | bytes 405512 | tf_op jit(solution)/shard_map/ppermute | solution.py:27
  9.1 7.4 %collective-permute-start.2 = (bf16[2,2,1,66,256]{4,3,2,1,0:T(8,128)(2,1)S(1)}, bf16[2,2,1,66,256]{4,3,2,1,0:T(8,128)(2,1)S(1)}, u32[]{:S(2)}, u32[]{:S(2)}) collective-permute-start(bf16[2,2,1,66,256]{4,3,2,1,0:T(8,128)(2,1)S(1)} %get-tuple-element.14), channel_id=1, source_target_pairs={{0,2},{2,4},{4,6},{6,8},{8,10},{10,12},{12,14},{14,16},{16,18},{18... | collective-permute-start | bytes 405512 | tf_op jit(solution)/shard_map/ppermute | solution.py:26
  20.1 2.9 %copy-start.5 = (bf16[9,256,256]{2,1,0:T(8,128)(2,1)S(1)}, bf16[9,256,256]{2,1,0:T(8,128)(2,1)}, u32[]{:S(2)}) copy-start(bf16[9,256,256]{2,1,0:T(8,128)(2,1)} %param.7) | copy-start | bytes 3538948
  21.0 19.6 %copy-start.7 = (bf16[1,2,6,64,256]{4,3,2,1,0:T(8,128)(2,1)}, bf16[1,2,6,64,256]{4,3,2,1,0:T(8,128)(2,1)S(1)}, u32[]{:S(2)}) copy-start(bf16[1,2,6,64,256]{4,3,2,1,0:T(8,128)(2,1)S(1)} %fusion.45) | copy-start | bytes 1179652
  21.0 19.5 %collective-permute-start.5 = (bf16[1,2,6,1,256]{4,3,2,1,0:T(2,128)(2,1)S(1)}, bf16[1,2,6,1,256]{4,3,2,1,0:T(2,128)(2,1)S(1)}, u32[]{:S(2)}, u32[]{:S(2)}) collective-permute-start(bf16[1,2,6,1,256]{4,3,2,1,0:T(2,128)(2,1)S(1)} %get-tuple-element.25), channel_id=1, source_target_pairs={{1,0},{0,1},{3,2},{2,3},{5,4},{4,5},{7,6},{6,7},{9,8},{8,9},{11,10... | collective-permute-start | bytes 18440 | tf_op jit(solution)/shard_map/ppermute | solution.py:27
  22.6 18.0 %collective-permute-start.4 = (bf16[1,2,6,1,256]{4,3,2,1,0:T(2,128)(2,1)S(1)}, bf16[1,2,6,1,256]{4,3,2,1,0:T(2,128)(2,1)S(1)}, u32[]{:S(2)}, u32[]{:S(2)}) collective-permute-start(bf16[1,2,6,1,256]{4,3,2,1,0:T(2,128)(2,1)S(1)} %get-tuple-element.24), channel_id=1, source_target_pairs={{0,1},{1,0},{2,3},{3,2},{4,5},{5,4},{6,7},{7,6},{8,9},{9,8},{10,11... | collective-permute-start | bytes 18440 | tf_op jit(solution)/shard_map/ppermute | solution.py:26
  26.0 4.7 %copy-start.9 = (bf16[2,6,64,256]{3,2,1,0:T(8,128)(2,1)}, bf16[2,6,64,256]{3,2,1,0:T(8,128)(2,1)S(1)}, u32[]{:S(2)}) copy-start(bf16[2,6,64,256]{3,2,1,0:T(8,128)(2,1)S(1)} %fusion.5) | copy-start | bytes 1179652
  26.4 19.3 %collective-permute-start.9 = (bf16[1,2,6,1,256]{4,3,2,1,0:T(2,128)(2,1)S(1)}, bf16[1,2,6,1,256]{4,3,2,1,0:T(2,128)(2,1)S(1)}, u32[]{:S(2)}, u32[]{:S(2)}) collective-permute-start(bf16[1,2,6,1,256]{4,3,2,1,0:T(2,128)(2,1)S(1)} %get-tuple-element.23), channel_id=1, source_target_pairs={{1,0},{0,1},{3,2},{2,3},{5,4},{4,5},{7,6},{6,7},{9,8},{8,9},{11,10... | collective-permute-start | bytes 18440 | tf_op jit(solution)/shard_map/ppermute | solution.py:27
  28.0 17.7 %collective-permute-start.8 = (bf16[1,2,6,1,256]{4,3,2,1,0:T(2,128)(2,1)S(1)}, bf16[1,2,6,1,256]{4,3,2,1,0:T(2,128)(2,1)S(1)}, u32[]{:S(2)}, u32[]{:S(2)}) collective-permute-start(bf16[1,2,6,1,256]{4,3,2,1,0:T(2,128)(2,1)S(1)} %get-tuple-element.22), channel_id=1, source_target_pairs={{0,1},{1,0},{2,3},{3,2},{4,5},{5,4},{6,7},{7,6},{8,9},{9,8},{10,11... | collective-permute-start | bytes 18440 | tf_op jit(solution)/shard_map/ppermute | solution.py:26
  35.1 60.6 %copy-start.1 = (bf16[2,6,64,256]{3,2,1,0:T(8,128)(2,1)S(1)}, bf16[2,6,64,256]{3,2,1,0:T(8,128)(2,1)}, u32[]{:S(2)}) copy-start(bf16[2,6,64,256]{3,2,1,0:T(8,128)(2,1)} %param.5) | copy-start | bytes 1179652
  35.2 74.4 %all-to-all-start = ((f32[1,9,256,256]{3,0,1,2:T(1,128)}), f32[1,9,256,256]{3,0,1,2:T(1,128)S(1)}, u32[]{:S(2)}, u32[]{:S(2)}) async-start(f32[1,9,256,256]{3,0,1,2:T(1,128)} %copy.14), calls=%async_computation | async-start | bytes 4718592 | tf_op jit(solution)/shard_map/all_to_all | solution.py:76
  40.6 52.2 %collective-permute-start.7 = (bf16[1,2,1,66,256]{4,3,2,1,0:T(8,128)(2,1)S(1)}, bf16[1,2,1,66,256]{4,3,2,1,0:T(8,128)(2,1)S(1)}, u32[]{:S(2)}, u32[]{:S(2)}) collective-permute-start(bf16[1,2,1,66,256]{4,3,2,1,0:T(8,128)(2,1)S(1)} %get-tuple-element.21), channel_id=1, source_target_pairs={{2,0},{4,2},{6,4},{8,6},{10,8},{12,10},{14,12},{16,14},{18,16},{20... | collective-permute-start | bytes 202760 | tf_op jit(solution)/shard_map/ppermute | solution.py:27
  43.7 50.8 %collective-permute-start.6 = (bf16[1,2,1,66,256]{4,3,2,1,0:T(8,128)(2,1)S(1)}, bf16[1,2,1,66,256]{4,3,2,1,0:T(8,128)(2,1)S(1)}, u32[]{:S(2)}, u32[]{:S(2)}) collective-permute-start(bf16[1,2,1,66,256]{4,3,2,1,0:T(8,128)(2,1)S(1)} %get-tuple-element.20), channel_id=1, source_target_pairs={{0,2},{2,4},{4,6},{6,8},{8,10},{10,12},{12,14},{14,16},{16,18},{18... | collective-permute-start | bytes 202760 | tf_op jit(solution)/shard_map/ppermute | solution.py:26
  45.7 47.1 %copy-start.11 = (bf16[1,2,6,1,256]{4,3,2,1,0:T(2,128)(2,1)}, bf16[1,2,6,1,256]{4,3,2,1,0:T(2,128)(2,1)S(1)}, u32[]{:S(2)}) copy-start(bf16[1,2,6,1,256]{4,3,2,1,0:T(2,128)(2,1)S(1)} %collective-permute-done.8) | copy-start | bytes 18436
  47.3 66.6 %collective-permute-start.11 = (bf16[1,2,1,66,256]{4,3,2,1,0:T(8,128)(2,1)}, bf16[1,2,1,66,256]{4,3,2,1,0:T(8,128)(2,1)S(1)}, u32[]{:S(2)}, u32[]{:S(2)}) collective-permute-start(bf16[1,2,1,66,256]{4,3,2,1,0:T(8,128)(2,1)} %get-tuple-element.19), channel_id=1, source_target_pairs={{2,0},{4,2},{6,4},{8,6},{10,8},{12,10},{14,12},{16,14},{18,16},{20... | collective-permute-start | bytes 202760 | tf_op jit(solution)/shard_map/ppermute | solution.py:27
  51.8 62.8 %collective-permute-start.10 = (bf16[1,2,1,66,256]{4,3,2,1,0:T(8,128)(2,1)S(1)}, bf16[1,2,1,66,256]{4,3,2,1,0:T(8,128)(2,1)}, u32[]{:S(2)}, u32[]{:S(2)}) collective-permute-start(bf16[1,2,1,66,256]{4,3,2,1,0:T(8,128)(2,1)S(1)} %get-tuple-element.18), channel_id=1, source_target_pairs={{0,2},{2,4},{4,6},{6,8},{8,10},{10,12},{12,14},{14,16},{16,18},{18... | collective-permute-start | bytes 202760 | tf_op jit(solution)/shard_map/ppermute | solution.py:26
  109.5 57.6 %all-to-all-start.2 = ((f32[16,1,9,16,256]{4,3,2,1,0:T(8,128)}), f32[16,1,9,16,256]{4,3,2,1,0:T(8,128)}, u32[]{:S(2)}, u32[]{:S(2)}) async-start(f32[16,1,9,16,256]{4,3,2,1,0:T(8,128)} %fusion.84), calls=%async_computation.2 | async-start | bytes 4718592 | tf_op jit(solution)/shard_map/all_to_all | solution.py:12
  113.9 3.1 %copy-start.4 = (bf16[9,256,256]{2,1,0:T(8,128)(2,1)S(1)}, bf16[9,256,256]{2,1,0:T(8,128)(2,1)}, u32[]{:S(2)}) copy-start(bf16[9,256,256]{2,1,0:T(8,128)(2,1)} %param.6) | copy-start | bytes 3538948
  113.9 3.4 %copy-start.6 = (bf16[9,256,256]{2,1,0:T(8,128)(2,1)S(1)}, bf16[9,256,256]{2,1,0:T(8,128)(2,1)}, u32[]{:S(2)}) copy-start(bf16[9,256,256]{2,1,0:T(8,128)(2,1)} %param.7) | copy-start | bytes 3538948
  113.9 0.6 copy-start.10
  118.7 1.0 copy-start
  131.4 41.3 %copy-start.8 = (f32[2,6,64,256]{3,2,1,0:T(8,128)S(1)}, f32[2,6,64,256]{3,2,1,0:T(8,128)}, u32[]{:S(2)}) copy-start(f32[2,6,64,256]{3,2,1,0:T(8,128)} %convolution_add_fusion.2) | copy-start | bytes 2359300
  167.1 17.7 %all-to-all-start.1 = ((f32[2,1,18432]{2,1,0:T(1,128)}), f32[2,1,18432]{2,1,0:T(1,128)}, u32[]{:S(2)}, u32[]{:S(2)}) async-start(f32[2,1,18432]{2,1,0:T(1,128)} %reshape.308), calls=%async_computation.1 | async-start | bytes 294912 | tf_op jit(solution)/shard_map/all_to_all | solution.py:84
  178.8 10.4 %copy-start.2 = (bf16[2,6,64,256]{3,2,1,0:T(8,128)(2,1)S(1)}, bf16[2,6,64,256]{3,2,1,0:T(8,128)(2,1)}, u32[]{:S(2)}) copy-start(bf16[2,6,64,256]{3,2,1,0:T(8,128)(2,1)} %param.5) | copy-start | bytes 1179652
  184.9 11.8 %all-to-all-start.3 = ((f32[2,1,18432]{2,1,0:T(1,128)}), f32[2,1,18432]{2,1,0:T(1,128)}, u32[]{:S(2)}, u32[]{:S(2)}) async-start(f32[2,1,18432]{2,1,0:T(1,128)} %reshape.310), calls=%async_computation.3 | async-start | bytes 294912 | tf_op jit(solution)/shard_map/all_to_all | solution.py:85
